TPU v7x, 128 devices: a whole 4x4x4 slice. The times are simulated.
128 devices in a mesh: dp: 16 (over x, z_hi, core), ctx: 8 (over z_lo, y).
Axes of the slice: x: 4, y: 4, z: 4 (z_hi: 2, z_lo: 2; z = z_hi * 2 + z_lo), core: 2. Of those that a mesh axis runs over, the one named last changes fastest.
Arguments:
- light_flux: float32 [16, 6, 4096], P('dp', None, 'ctx'), may hold values from -6 to 6
- lengths: int32 [16], P('dp'), may hold values from 1024 to 4096, as said below
- offsets: int32 [16, 4096], P('dp', 'ctx'), may hold values from 0 to 3
- start_weight: float32 [512, 3], replicated, may hold values from -3.5 to 3.5
- conv_weight: bfloat16 [2, 1024, 1536], P(None, 'dp'), may hold values from -0.15625 to 0.15625
- gate_bias: float32 [2, 1024], replicated, may hold values from -4 to 4
- mix_first: bfloat16 [1024, 512], P('dp'), may hold values from -0.25 to 0.25
- mix_last: bfloat16 [512, 512], P('dp'), may hold values from -0.25 to 0.25
- end_weight: float32 [6, 512], replicated, may hold values from -0.25 to 0.25
- cotangent: float32 [16, 3, 4096], P('dp', None, 'ctx'), may hold values from -0.0234375 to 0.0234375
Outputs:
- coupled: float32 [16, 3, 4096], P('dp', None, 'ctx')
- grad_start: float32 [512, 3], replicated
- grad_conv: float32 [2, 1024, 1536], P(None, 'dp')
- grad_bias: float32 [2, 1024], replicated
- grad_mix_first: float32 [1024, 512], P('dp')
- grad_mix_last: float32 [512, 512], P('dp')
- grad_end: float32 [6, 512], replicated
Inputs may be any that keep to these rules, and one draw needn't show every extreme that they name: `lengths`: epochs at or past a curve's length are padding; at least one curve has no padding.
All inputs are finite; a program needn't handle non-finite values.
Results may differ from a plain program's by a relative error of at most 0.0091.
Values may be sent and summed in bfloat16 or wider, within the bound.
No kernel may reach another device: no remote copies, remote signals or barrier semaphores. Data moves between devices by JAX's collectives and lax.ppermute only.
A program may use at most 128 MiB of HBM per device.

v0:
```python
import jax
import jax.numpy as jnp
from jax import lax
from jax.sharding import PartitionSpec as P

BUCKETS = 4
highest = lax.Precision.HIGHEST


def from_behind(array, axis, by):
    size = lax.axis_size(axis)
    pairs = [(i, i + by) for i in range(size) if 0 <= i + by < size]
    return lax.ppermute(array, axis, pairs)


def tap_stack(padded, bucket, dilation, reach_len, col_count):
    centre = lax.slice_in_dim(padded, reach_len, reach_len + col_count, axis=1)
    left_tap = lax.slice_in_dim(
        padded, reach_len - dilation, reach_len - dilation + col_count, axis=1
    )
    right_tap = lax.slice_in_dim(
        padded, reach_len + dilation, reach_len + dilation + col_count, axis=1
    )
    for shift_k in range(1, BUCKETS):
        chosen = (bucket == shift_k)[None, :]
        left_start = reach_len - dilation - shift_k
        right_start = reach_len + dilation + shift_k
        left_tap = jnp.where(
            chosen, lax.slice_in_dim(padded, left_start, left_start + col_count, axis=1), left_tap
        )
        right_tap = jnp.where(
            chosen,
            lax.slice_in_dim(padded, right_start, right_start + col_count, axis=1),
            right_tap,
        )
    return jnp.concatenate([left_tap, centre, right_tap], axis=0)


def place_piece(piece, start_col, total_len):
    return jnp.pad(piece, ((0, 0), (start_col, total_len - start_col - piece.shape[1])))


def tap_transpose(d_stacked, bucket, dilation, reach_len, col_count, channels):
    total_len = col_count + 2 * reach_len
    d_left = d_stacked[:channels]
    d_centre = d_stacked[channels : 2 * channels]
    d_right = d_stacked[2 * channels :]
    window = place_piece(d_centre, reach_len, total_len)
    for shift_k in range(BUCKETS):
        chosen = (bucket == shift_k)[None, :]
        left_part = jnp.where(chosen, d_left, 0.0)
        right_part = jnp.where(chosen, d_right, 0.0)
        window = window + place_piece(left_part, reach_len - dilation - shift_k, total_len)
        window = window + place_piece(right_part, reach_len + dilation + shift_k, total_len)
    return window


def gate_forward(preact):
    channels = preact.shape[0] // 2
    return jnp.tanh(preact[:channels]) * jax.nn.sigmoid(preact[channels:])


def gate_backward(preact, d_gated):
    channels = preact.shape[0] // 2
    tangent = jnp.tanh(preact[:channels])
    sigmoid_part = jax.nn.sigmoid(preact[channels:])
    d_upper = d_gated * sigmoid_part * (1.0 - tangent * tangent)
    d_lower = d_gated * tangent * sigmoid_part * (1.0 - sigmoid_part)
    return jnp.concatenate([d_upper, d_lower], axis=0).astype(jnp.bfloat16)


def contract_rows(left_op, right_op, precision=None):
    return lax.dot_general(
        left_op,
        right_op,
        (((1,), (1,)), ((), ())),
        precision=precision,
        preferred_element_type=jnp.float32,
    )


def contract_cols(left_op, right_op, precision=None):
    return lax.dot_general(
        left_op,
        right_op,
        (((0,), (0,)), ((), ())),
        precision=precision,
        preferred_element_type=jnp.float32,
    )


def extend(hidden, reach_len, shard_len):
    pieces_low = []
    pieces_high = []
    remain = reach_len
    distance = 1
    while remain > 0:
        amount = min(shard_len, remain)
        from_low = from_behind(hidden[:, shard_len - amount :], "ctx", distance)
        from_high = from_behind(hidden[:, :amount], "ctx", -distance)
        pieces_low.insert(0, from_low)
        pieces_high.append(from_high)
        remain = remain - amount
        distance = distance + 1
    return jnp.concatenate(pieces_low + [hidden] + pieces_high, axis=1)


def return_rims(grad_window, reach_len, shard_len):
    middle = grad_window[:, reach_len : reach_len + shard_len]
    remain = reach_len
    distance = 1
    end_col = reach_len
    while remain > 0:
        amount = min(shard_len, remain)
        piece_low = grad_window[:, end_col - amount : end_col]
        high_start = reach_len + shard_len + (reach_len - remain)
        piece_high = grad_window[:, high_start : high_start + amount]
        back_low = from_behind(piece_low, "ctx", -distance)
        back_high = from_behind(piece_high, "ctx", distance)
        middle = middle + place_piece(back_low, shard_len - amount, shard_len)
        middle = middle + place_piece(back_high, 0, shard_len)
        end_col = end_col - amount
        remain = remain - amount
        distance = distance + 1
    return middle


def layer_forward(conv_shard, mix_shard, bias_row, stacked):
    full_conv, full_mix = (
        lax.all_gather(conv_shard, "dp", axis=0, tiled=True),
        lax.all_gather(mix_shard, "dp", axis=0, tiled=True),
    )
    preact = jnp.dot(full_conv, stacked, preferred_element_type=jnp.float32) + bias_row[:, None]
    gated = gate_forward(preact).astype(jnp.bfloat16)
    mixed_rows = jnp.dot(full_mix, gated, preferred_element_type=jnp.float32)
    return (preact, gated, mixed_rows, (full_conv, full_mix))


def mix_back(mix_weight, d_mixed):
    return contract_cols(mix_weight, d_mixed)


def conv_back(conv_weight_rows, dz_rows):
    return contract_cols(conv_weight_rows, dz_rows)


def reduce_grad(left_op, right_op):
    full_grad = contract_rows(left_op, right_op)
    summed = lax.psum(full_grad, "ctx")
    return lax.psum_scatter(summed, "dp", scatter_dimension=0, tiled=True)


def local(
    light_flux,
    lengths,
    offsets,
    start_weight,
    conv_weight,
    gate_bias,
    mix_first,
    mix_last,
    end_weight,
    cotangent,
):
    shard_len = light_flux.shape[2]
    half_bands = light_flux.shape[1] // 2
    channels = start_weight.shape[0]
    position = lax.axis_index("ctx") * shard_len + jnp.arange(shard_len, dtype=jnp.int32)
    valid_mask = (position < lengths[0]).astype(jnp.float32)
    bucket = offsets[0]
    first_half = light_flux[0, :half_bands]
    second_half = light_flux[0, half_bands:]
    dilations = (shard_len // 4, shard_len + shard_len // 2)
    reaches = (dilations[0] + BUCKETS - 1, dilations[1] + BUCKETS - 1)
    hidden_first = (jnp.dot(start_weight, first_half, precision=highest) * valid_mask).astype(
        jnp.bfloat16
    )
    stacked_first = tap_stack(
        extend(hidden_first, reaches[0], shard_len), bucket, dilations[0], reaches[0], shard_len
    )
    pre_first, gated_first, mixed_first, kept_first = layer_forward(
        conv_weight[0], mix_first, gate_bias[0], stacked_first
    )
    hidden_second = (
        (hidden_first.astype(jnp.float32) + mixed_first[:channels]) * valid_mask
    ).astype(jnp.bfloat16)
    stacked_second = tap_stack(
        extend(hidden_second, reaches[1], shard_len), bucket, dilations[1], reaches[1], shard_len
    )
    pre_second, gated_second, mixed_second, kept_second = layer_forward(
        conv_weight[1], mix_last, gate_bias[1], stacked_second
    )
    skip_total = mixed_first[channels:] + mixed_second
    end_out = jnp.dot(end_weight, skip_total, precision=highest)
    growth = jnp.exp(end_out[:half_bands])
    coupled = ((growth * second_half + end_out[half_bands:]) * valid_mask)[None]
    d_coupled = cotangent[0] * valid_mask
    d_end = jnp.concatenate([d_coupled * growth * second_half, d_coupled], axis=0)
    grad_end_local = contract_rows(d_end, skip_total, highest)
    d_skip = contract_cols(end_weight, d_end, highest)
    d_skip_b = d_skip.astype(jnp.bfloat16)
    d_gated_second = mix_back(kept_second[1], d_skip_b)
    grad_mix_last = reduce_grad(d_skip_b, gated_second)
    dz_second = gate_backward(pre_second, d_gated_second)
    grad_conv_second = reduce_grad(dz_second, stacked_second)
    bias_second = jnp.sum(dz_second.astype(jnp.float32), axis=1)
    d_stacked_second = conv_back(kept_second[0], dz_second)
    d_window_second = tap_transpose(
        d_stacked_second, bucket, dilations[1], reaches[1], shard_len, channels
    )
    d_field_second = return_rims(d_window_second, reaches[1], shard_len)
    d_mixed_first = jnp.concatenate([d_field_second * valid_mask, d_skip], axis=0).astype(
        jnp.bfloat16
    )
    d_gated_first = mix_back(kept_first[1], d_mixed_first)
    grad_mix_first = reduce_grad(d_mixed_first, gated_first)
    dz_first = gate_backward(pre_first, d_gated_first)
    grad_conv_first = reduce_grad(dz_first, stacked_first)
    bias_first = jnp.sum(dz_first.astype(jnp.float32), axis=1)
    d_stacked_first = conv_back(kept_first[0], dz_first)
    d_window_first = tap_transpose(
        d_stacked_first, bucket, dilations[0], reaches[0], shard_len, channels
    )
    d_hidden_first = d_field_second * valid_mask + return_rims(
        d_window_first, reaches[0], shard_len
    )
    grad_start_local = contract_rows(d_hidden_first * valid_mask, first_half, highest)
    grad_start, grad_bias, grad_end = lax.psum(
        (grad_start_local, jnp.stack([bias_first, bias_second]), grad_end_local), ("dp", "ctx")
    )
    grad_conv = jnp.stack([grad_conv_first, grad_conv_second])
    return (coupled, grad_start, grad_conv, grad_bias, grad_mix_first, grad_mix_last, grad_end)


def solution(mesh):
    in_specs = (
        P("dp", None, "ctx"),
        P("dp"),
        P("dp", "ctx"),
        P(),
        P(None, "dp", None),
        P(),
        P("dp", None),
        P("dp", None),
        P(),
        P("dp", None, "ctx"),
    )
    out_specs = (
        P("dp", None, "ctx"),
        P(),
        P(None, "dp", None),
        P(),
        P("dp", None),
        P("dp", None),
        P(),
    )
    return jax.shard_map(local, mesh=mesh, in_specs=in_specs, out_specs=out_specs, check_vma=False)
```

profile of v0, /device:TPU:1, one launch (start us, length us, event | category | flops | bytes accessed | tf_op | source)
XLA Modules:
  0.0 635.6 jit_solution(13438480193903545730)
XLA Ops:
  13.8 4.0 collective-permute-start
  20.1 3.8 collective-permute-done.1
  23.9 4.0 fusion.43
  28.0 39.5 %all-gather.8.cloned.1.call-done = bf16[1,1024,1536]{2,1,0:T(8,128)(2,1)} async-done(((bf16[1,64,1536]{2,1,0:T(8,128)(2,1)}), bf16[1,1024,1536]{2,1,0:T(8,128)(2,1)}) %all-gather.8.cloned.1.call-update) | async-done | bytes 3145744 | tf_op jit(solution)/shard_map/all_gather | solution.py:130
  67.5 3.7 add_bitcast_fusion.1
  73.0 40.6 %all-gather.6.cloned.1.call-done = bf16[1024,512]{1,0:T(8,128)(2,1)} async-done(((bf16[64,512]{1,0:T(8,128)(2,1)}), bf16[1024,512]{1,0:T(8,128)(2,1)}) %all-gather.6.cloned.1.call-update) | async-done | bytes 1048592 | tf_op jit(solution)/shard_map/all_gather | solution.py:131
  117.1 4.0 collective-permute-start.3
  121.2 4.6 collective-permute-start.2
  127.1 36.2 %all_gather.15 = bf16[512,512]{1,0:T(8,128)(2,1)} all-gather(bf16[32,512]{1,0:T(8,128)(2,1)S(1)} %copy-done.31), channel_id=1, replica_groups=mesh['dp'=16,'ctx'=8] {'dp'}, dimensions={0}, use_global_device_ids=true | all-gather | bytes 557056 | tf_op jit(solution)/shard_map/all_gather | solution.py:131
  166.2 13.4 %all-gather.10.cloned.1.call-done = bf16[1,1024,1536]{2,1,0:T(8,128)(2,1)} async-done(((bf16[1,64,1536]{2,1,0:T(8,128)(2,1)}), bf16[1,1024,1536]{2,1,0:T(8,128)(2,1)}) %all-gather.10.cloned.1.call-update) | async-done | bytes 3145744 | tf_op jit(solution)/shard_map/all_gather | solution.py:130
  179.6 3.9 add_bitcast_fusion
  198.2 5.0 collective-permute-start.7
  207.4 5.7 collective-permute-start.9
  213.1 26.5 %collective-permute-done.8 = f32[512,259]{0,1:T(8,128)S(1)} collective-permute-done((f32[512,259]{0,1:T(8,128)S(1)}, f32[512,259]{0,1:T(8,128)S(1)}, u32[]{:S(2)}, u32[]{:S(2)}) %collective-permute-start.8) | collective-permute-done | bytes 530464 | tf_op jit(solution)/shard_map/ppermute | solution.py:13
  239.5 2.9 fusion.76
  245.4 5.7 fusion.32
  256.2 4.5 fusion.33
  261.9 3.7 convolution_bitcast_fusion
  267.7 10.9 %reduce-scatter.11.cloned.1.call-done = f32[32,512]{1,0:T(8,128)} async-done(((f32[512,512]{1,0:T(8,128)}), f32[32,512]{1,0:T(8,128)}) %reduce-scatter.11.cloned.1.call-update) | async-done | bytes 65552 | tf_op jit(solution)/shard_map/reduce_scatter | solution.py:150
  278.6 74.3 %reduce-scatter.9.cloned.1.call-done = f32[64,512]{1,0:T(8,128)} async-done(((f32[1024,512]{1,0:T(8,128)}), f32[64,512]{1,0:T(8,128)}) %reduce-scatter.9.cloned.1.call-update) | async-done | bytes 131088 | tf_op jit(solution)/shard_map/reduce_scatter | solution.py:150
  352.9 93.9 %reduce-scatter.7.cloned.1.call-done = f32[64,1536]{1,0:T(8,128)} async-done(((f32[1024,1536]{1,0:T(8,128)}), f32[64,1536]{1,0:T(8,128)}) %reduce-scatter.7.cloned.1.call-update) | async-done | bytes 393232 | tf_op jit(solution)/shard_map/reduce_scatter | solution.py:150
  446.8 93.0 %reduce-scatter.5.cloned.1.call-done = f32[64,1536]{1,0:T(8,128)} async-done(((f32[1024,1536]{1,0:T(8,128)}), f32[64,1536]{1,0:T(8,128)}) %reduce-scatter.5.cloned.1.call-update) | async-done | bytes 393232 | tf_op jit(solution)/shard_map/reduce_scatter | solution.py:150
  541.3 4.0 collective-permute-start.11
  549.9 73.7 %all-reduce.22 = (f32[512,3]{0,1:T(4,128)}, f32[2,1024]{1,0:T(2,128)}, f32[6,512]{1,0:T(8,128)}) all-reduce(f32[512,3]{0,1:T(4,128)S(1)} %fusion.15, f32[2,1024]{1,0:T(2,128)S(1)} %pad_maximum_fusion.22, f32[6,512]{1,0:T(8,128)S(1)} %fusion.55), channel_id=1, replica_groups=mesh['dp'=16,'ctx'=8] {'dp','ctx'}, use_global_device_ids=true, to_apply=%region_0.1 | all-reduce | flops 6656 | bytes 53248 | tf_op jit(solution)/shard_map/psum | solution.py:228
  (145 shorter events, 58.7 us)
Async XLA Ops:
  7.2 177.9 %copy-start = (f32[6,512]{1,0:T(8,128)S(1)}, f32[6,512]{1,0:T(8,128)}, u32[]{:S(2)}) copy-start(f32[6,512]{1,0:T(8,128)} %param.18) | copy-start | bytes 36868
  7.2 60.3 %all-gather.8.cloned.1.call-start = ((), (), s32[]{:S(2)}) async-start(), calls=%async_computation.5 | async-start | bytes 3342336 | tf_op jit(solution)/shard_map/all_gather | solution.py:130
  9.1 104.5 %all-gather.6.cloned.1.call-start = ((), (), s32[]{:S(2)}) async-start(), calls=%async_computation.4 | async-start | bytes 1114112 | tf_op jit(solution)/shard_map/all_gather | solution.py:131
  9.8 169.8 %all-gather.10.cloned.1.call-start = ((), (), s32[]{:S(2)}) async-start(), calls=%async_computation.6 | async-start | bytes 3342336 | tf_op jit(solution)/shard_map/all_gather | solution.py:130
  10.6 268.1 %reduce-scatter.11.cloned.1.call-start = ((), (), s32[]{:S(2)}) async-start(), calls=%async_computation.10 | async-start | bytes 1114112 | tf_op jit(solution)/shard_map/reduce_scatter | solution.py:150
  13.7 101.8 %copy-start.3 = (bf16[512,512]{0,1:T(8,128)(2,1)}, bf16[512,512]{0,1:T(8,128)(2,1)S(1)}, u32[]{:S(2)}) copy-start(bf16[512,512]{0,1:T(8,128)(2,1)S(1)} %fusion.11) | copy-start | bytes 1572868
  13.8 6.4 collective-permute-start
  17.8 6.1 collective-permute-start.1
  115.8 47.5 %collective-permute-start.4 = (bf16[512,512]{0,1:T(8,128)(2,1)S(1)}, bf16[512,512]{0,1:T(8,128)(2,1)S(1)}, u32[]{:S(2)}, u32[]{:S(2)}) collective-permute-start(bf16[512,512]{0,1:T(8,128)(2,1)S(1)} %fusion.25), channel_id=1, source_target_pairs={{1,0},{2,1},{3,2},{4,3},{5,4},{6,5},{7,6},{9,8},{10,9},{11,10},{12... | collective-permute-start | bytes 1572872 | tf_op jit(solution)/shard_map/ppermute | solution.py:13
  117.1 46.3 %collective-permute-start.3 = (bf16[512,512]{0,1:T(8,128)(2,1)S(1)}, bf16[512,512]{0,1:T(8,128)(2,1)S(1)}, u32[]{:S(2)}, u32[]{:S(2)}) collective-permute-start(bf16[512,512]{0,1:T(8,128)(2,1)S(1)} %fusion.25), channel_id=1, source_target_pairs={{0,1},{1,2},{2,3},{3,4},{4,5},{5,6},{6,7},{8,9},{9,10},{10,11},{11... | collective-permute-start | bytes 1572872 | tf_op jit(solution)/shard_map/ppermute | solution.py:13
  121.2 42.2 %collective-permute-start.2 = (bf16[512,259]{0,1:T(8,128)(2,1)S(1)}, bf16[512,259]{0,1:T(8,128)(2,1)S(1)}, u32[]{:S(2)}, u32[]{:S(2)}) collective-permute-start(bf16[512,259]{0,1:T(8,128)(2,1)S(1)} %get-tuple-element.71), channel_id=1, source_target_pairs={{0,2},{1,3},{2,4},{3,5},{4,6},{5,7},{8,10},{9,11},{10,12},{11,13},... | collective-permute-start | bytes 795656 | tf_op jit(solution)/shard_map/ppermute | solution.py:13
  125.8 37.6 %collective-permute-start.5 = (bf16[512,259]{0,1:T(8,128)(2,1)S(1)}, bf16[512,259]{0,1:T(8,128)(2,1)S(1)}, u32[]{:S(2)}, u32[]{:S(2)}) collective-permute-start(bf16[512,259]{0,1:T(8,128)(2,1)S(1)} %get-tuple-element.72), channel_id=1, source_target_pairs={{2,0},{3,1},{4,2},{5,3},{6,4},{7,5},{10,8},{11,9},{12,10},{13,11},... | collective-permute-start | bytes 795656 | tf_op jit(solution)/shard_map/ppermute | solution.py:13
  197.0 42.6 %collective-permute-start.6 = (f32[512,512]{0,1:T(8,128)}, f32[512,512]{0,1:T(8,128)S(1)}, u32[]{:S(2)}, u32[]{:S(2)}) collective-permute-start(f32[512,512]{0,1:T(8,128)} %get-tuple-element.27), channel_id=1, source_target_pairs={{1,0},{2,1},{3,2},{4,3},{5,4},{6,5},{7,6},{9,8},{10,9},{11,10},{12... | collective-permute-start | bytes 3145736 | tf_op jit(solution)/shard_map/ppermute | solution.py:13
  198.2 41.3 %collective-permute-start.7 = (f32[512,512]{0,1:T(8,128)}, f32[512,512]{0,1:T(8,128)}, u32[]{:S(2)}, u32[]{:S(2)}) collective-permute-start(f32[512,512]{0,1:T(8,128)} %get-tuple-element.28), channel_id=1, source_target_pairs={{0,1},{1,2},{2,3},{3,4},{4,5},{5,6},{6,7},{8,9},{9,10},{10,11},{11... | collective-permute-start | bytes 3145736 | tf_op jit(solution)/shard_map/ppermute | solution.py:13
  204.7 148.2 %reduce-scatter.9.cloned.1.call-start = ((), (), s32[]{:S(2)}) async-start(), calls=%async_computation.9 | async-start | bytes 2228224 | tf_op jit(solution)/shard_map/reduce_scatter | solution.py:150
  206.1 33.4 %collective-permute-start.8 = (f32[512,259]{0,1:T(8,128)S(1)}, f32[512,259]{0,1:T(8,128)S(1)}, u32[]{:S(2)}, u32[]{:S(2)}) collective-permute-start(f32[512,259]{0,1:T(8,128)S(1)} %get-tuple-element.29), channel_id=1, source_target_pairs={{2,0},{3,1},{4,2},{5,3},{6,4},{7,5},{10,8},{11,9},{12,10},{13,11},... | collective-permute-start | bytes 1591304 | tf_op jit(solution)/shard_map/ppermute | solution.py:13
  207.4 32.1 %collective-permute-start.9 = (f32[512,259]{0,1:T(8,128)S(1)}, f32[512,259]{0,1:T(8,128)S(1)}, u32[]{:S(2)}, u32[]{:S(2)}) collective-permute-start(f32[512,259]{0,1:T(8,128)S(1)} %get-tuple-element.30), channel_id=1, source_target_pairs={{0,2},{1,3},{2,4},{3,5},{4,6},{5,7},{8,10},{9,11},{10,12},{11,13},... | collective-permute-start | bytes 1591304 | tf_op jit(solution)/shard_map/ppermute | solution.py:13
  245.3 201.5 %reduce-scatter.7.cloned.1.call-start = ((), (), s32[]{:S(2)}) async-start(), calls=%async_computation.8 | async-start | bytes 6684672 | tf_op jit(solution)/shard_map/reduce_scatter | solution.py:150
  251.2 288.6 %reduce-scatter.5.cloned.1.call-start = ((), (), s32[]{:S(2)}) async-start(), calls=%async_computation.7 | async-start | bytes 6684672 | tf_op jit(solution)/shard_map/reduce_scatter | solution.py:150
  260.8 362.9 %all-reduce.26.cloned.1.call-start = ((), (), s32[]{:S(2)}) async-start(), calls=%async_computation.11 | async-start | bytes 1966080 | tf_op jit(solution)/shard_map/psum | solution.py:149
  267.7 278.9 %copy-start.17 = (bf16[512,512]{0,1:T(8,128)(2,1)S(1)}, bf16[512,512]{0,1:T(8,128)(2,1)}, u32[]{:S(2)}) copy-start(bf16[512,512]{0,1:T(8,128)(2,1)} %copy-done.16) | copy-start | bytes 1572868
  539.9 8.3 %collective-permute-start.10 = (f32[512,131]{0,1:T(8,128)S(1)}, f32[512,131]{0,1:T(8,128)S(1)}, u32[]{:S(2)}, u32[]{:S(2)}) collective-permute-start(f32[512,131]{0,1:T(8,128)S(1)} %get-tuple-element.67), channel_id=1, source_target_pairs={{1,0},{2,1},{3,2},{4,3},{5,4},{6,5},{7,6},{9,8},{10,9},{11,10},{12... | collective-permute-start | bytes 804872 | tf_op jit(solution)/shard_map/ppermute | solution.py:13
  541.3 7.7 %collective-permute-start.11 = (f32[512,131]{0,1:T(8,128)S(1)}, f32[512,131]{0,1:T(8,128)S(1)}, u32[]{:S(2)}, u32[]{:S(2)}) collective-permute-start(f32[512,131]{0,1:T(8,128)S(1)} %get-tuple-element.68), channel_id=1, source_target_pairs={{0,1},{1,2},{2,3},{3,4},{4,5},{5,6},{6,7},{8,9},{9,10},{10,11},{11... | collective-permute-start | bytes 804872 | tf_op jit(solution)/shard_map/ppermute | solution.py:13
  549.1 79.7 %copy-start.1 = (f32[6,512]{1,0:T(8,128)S(1)}, f32[6,512]{1,0:T(8,128)}, u32[]{:S(2)}) copy-start(f32[6,512]{1,0:T(8,128)} %param.18) | copy-start | bytes 36868
  (32 other events, 345.2 us)
Sparse Core Ops, SparseCore 0:
  11.0 56.4 all-gather.7
  69.9 43.6 all-gather.5
  116.0 63.5 all-gather.9
  204.8 73.7 reduce-scatter.10
  282.9 69.9 reduce-scatter.8
  357.5 89.2 reduce-scatter.6
  451.5 88.2 reduce-scatter.4
  542.8 71.9 all-reduce.25
where the time goes:
time: 637 us; the launch traced here: 636 us
  waiting for transfers between devices  400 us (63%)
  blocking collectives  110 us (17%)
  matrix products  38.1 us (6%)
  starting transfers between devices  35.7 us (6%)
  local copies, waits for them, and re-layouts  18.5 us (3%)
  other arithmetic  17.6 us (3%)
  between operations  15.4 us (2%)
    reduce_scatter x4, waiting for transfers between devices, reduce_grad(): return lax.psum_scatter(summed, 'dp', scatter_dimension=0, tiled=True)  272 us
    psum x1, blocking collectives, local(): lax.psum((grad_start_local, jnp.stack([bias_first, bias_second]), grad_en...  73.7 us
    all_gather x2, waiting for transfers between devices, layer_forward(): lax.all_gather(conv_shard, 'dp', axis=0, tiled=True)  52.9 us
    all_gather x1, waiting for transfers between devices, layer_forward(): lax.all_gather(mix_shard, 'dp', axis=0, tiled=True)  40.6 us
    all_gather x1, blocking collectives, layer_forward(): lax.all_gather(mix_shard, 'dp', axis=0, tiled=True)  36.2 us
    ppermute x12, starting transfers between devices, from_behind(): return lax.ppermute(array, axis, pairs)  35.2 us
    ppermute x12, waiting for transfers between devices, from_behind(): return lax.ppermute(array, axis, pairs)  33.3 us
    dot_general x6, matrix products, contract_rows(): lax.dot_general(left_op, right_op, (((1,), (1,)), ((), ())), precision=pr...  15.2 us
  transfers between devices with their start and end apart: 20, of which 12 were waited for; matrix products, arithmetic and copies ran while one was open for 7% of the time, Pallas kernels for 0%

commit v1 on v0

--- a/solution.py
+++ b/solution.py
@@ -226,7 +226,8 @@
     )
     grad_start_local = contract_rows(d_hidden_first * valid_mask, first_half, highest)
     grad_start, grad_bias, grad_end = lax.psum(
-        (grad_start_local, jnp.stack([bias_first, bias_second]), grad_end_local), ("dp", "ctx")
+        lax.psum((grad_start_local, jnp.stack([bias_first, bias_second]), grad_end_local), "dp"),
+        "ctx",
     )
     grad_conv = jnp.stack([grad_conv_first, grad_conv_second])
     return (coupled, grad_start, grad_conv, grad_bias, grad_mix_first, grad_mix_last, grad_end)

time: 637 us -> 668 us (1.049)
  the two profiles are of different devices: /device:TPU:1 before, /device:TPU:32 now
where the time goes in v1:
time: 668 us; the launch traced here: 667 us
  waiting for transfers between devices  411 us (62%)
  blocking collectives  120 us (18%)
  starting transfers between devices  46.5 us (7%)
  matrix products  38.1 us (6%)
  local copies, waits for them, and re-layouts  18.5 us (3%)
  other arithmetic  17.5 us (3%)
  between operations  15.4 us (2%)
    reduce_scatter x4, waiting for transfers between devices, reduce_grad(): return lax.psum_scatter(summed, 'dp', scatter_dimension=0, tiled=True)  258 us
    psum x1, blocking collectives, local(): lax.psum((grad_start_local, jnp.stack([bias_first, bias_second]), grad_en...  65.1 us
    all_gather x2, waiting for transfers between devices, layer_forward(): lax.all_gather(conv_shard, 'dp', axis=0, tiled=True)  58.2 us
    ppermute x12, waiting for transfers between devices, from_behind(): return lax.ppermute(array, axis, pairs)  53 us
    ppermute x12, starting transfers between devices, from_behind(): return lax.ppermute(array, axis, pairs)  46 us
    all_gather x1, waiting for transfers between devices, layer_forward(): lax.all_gather(mix_shard, 'dp', axis=0, tiled=True)  40.6 us
    psum x1, blocking collectives, local(): lax.psum(lax.psum((grad_start_local, jnp.stack([bias_first, bias_second])...  31.3 us
    all_gather x1, blocking collectives, layer_forward(): lax.all_gather(mix_shard, 'dp', axis=0, tiled=True)  23.5 us
  transfers between devices with their start and end apart: 20, of which 13 were waited for; matrix products, arithmetic and copies ran while one was open for 7% of the time, Pallas kernels for 0%

profile of v1, /device:TPU:32, one launch (start us, length us, event | category | flops | bytes accessed | tf_op | source)
XLA Modules:
  0.0 667.4 jit_solution(110341091393774015)
XLA Ops:
  17.2 4.5 collective-permute-start.1
  24.3 4.0 fusion.43
  28.4 36.6 %all-gather.8.cloned.1.call-done = bf16[1,1024,1536]{2,1,0:T(8,128)(2,1)} async-done(((bf16[1,64,1536]{2,1,0:T(8,128)(2,1)}), bf16[1,1024,1536]{2,1,0:T(8,128)(2,1)}) %all-gather.8.cloned.1.call-update) | async-done | bytes 3145744 | tf_op jit(solution)/shard_map/all_gather | solution.py:130
  65.0 3.7 add_bitcast_fusion.1
  70.5 40.6 %all-gather.6.cloned.1.call-done = bf16[1024,512]{1,0:T(8,128)(2,1)} async-done(((bf16[64,512]{1,0:T(8,128)(2,1)}), bf16[1024,512]{1,0:T(8,128)(2,1)}) %all-gather.6.cloned.1.call-update) | async-done | bytes 1048592 | tf_op jit(solution)/shard_map/all_gather | solution.py:131
  113.2 5.5 collective-permute-start.4
  124.1 4.8 collective-permute-start.5
  129.0 23.5 %all_gather.15 = bf16[512,512]{1,0:T(8,128)(2,1)} all-gather(bf16[32,512]{1,0:T(8,128)(2,1)S(1)} %copy-done.31), channel_id=1, replica_groups=mesh['dp'=16,'ctx'=8] {'dp'}, dimensions={0}, use_global_device_ids=true | all-gather | bytes 557056 | tf_op jit(solution)/shard_map/all_gather | solution.py:131
  155.4 21.7 %all-gather.10.cloned.1.call-done = bf16[1,1024,1536]{2,1,0:T(8,128)(2,1)} async-done(((bf16[1,64,1536]{2,1,0:T(8,128)(2,1)}), bf16[1,1024,1536]{2,1,0:T(8,128)(2,1)}) %all-gather.10.cloned.1.call-update) | async-done | bytes 3145744 | tf_op jit(solution)/shard_map/all_gather | solution.py:130
  177.1 3.9 add_bitcast_fusion
  194.4 5.4 collective-permute-start.6
  204.6 4.2 collective-permute-start.8
  212.2 26.0 %collective-permute-done.8 = f32[512,259]{0,1:T(8,128)S(1)} collective-permute-done((f32[512,259]{0,1:T(8,128)S(1)}, f32[512,259]{0,1:T(8,128)S(1)}, u32[]{:S(2)}, u32[]{:S(2)}) %collective-permute-start.8) | collective-permute-done | bytes 530464 | tf_op jit(solution)/shard_map/ppermute | solution.py:13
  238.1 12.4 %collective-permute-done.9 = f32[512,259]{0,1:T(8,128)S(1)} collective-permute-done((f32[512,259]{0,1:T(8,128)S(1)}, f32[512,259]{0,1:T(8,128)S(1)}, u32[]{:S(2)}, u32[]{:S(2)}) %collective-permute-start.9) | collective-permute-done | bytes 530464 | tf_op jit(solution)/shard_map/ppermute | solution.py:13
  258.3 5.7 fusion.32
  269.1 4.5 fusion.33
  274.8 3.7 convolution_bitcast_fusion
  280.7 72.1 %reduce-scatter.9.cloned.1.call-done = f32[64,512]{1,0:T(8,128)} async-done(((f32[1024,512]{1,0:T(8,128)}), f32[64,512]{1,0:T(8,128)}) %reduce-scatter.9.cloned.1.call-update) | async-done | bytes 131088 | tf_op jit(solution)/shard_map/reduce_scatter | solution.py:150
  352.8 93.1 %reduce-scatter.7.cloned.1.call-done = f32[64,1536]{1,0:T(8,128)} async-done(((f32[1024,1536]{1,0:T(8,128)}), f32[64,1536]{1,0:T(8,128)}) %reduce-scatter.7.cloned.1.call-update) | async-done | bytes 393232 | tf_op jit(solution)/shard_map/reduce_scatter | solution.py:150
  445.9 92.9 %reduce-scatter.5.cloned.1.call-done = f32[64,1536]{1,0:T(8,128)} async-done(((f32[1024,1536]{1,0:T(8,128)}), f32[64,1536]{1,0:T(8,128)}) %reduce-scatter.5.cloned.1.call-update) | async-done | bytes 393232 | tf_op jit(solution)/shard_map/reduce_scatter | solution.py:150
  538.9 5.6 collective-permute-start.10
  549.2 9.1 %collective-permute-done.11 = f32[512,131]{0,1:T(8,128)S(1)} collective-permute-done((f32[512,131]{0,1:T(8,128)S(1)}, f32[512,131]{0,1:T(8,128)S(1)}, u32[]{:S(2)}, u32[]{:S(2)}) %collective-permute-start.11) | collective-permute-done | bytes 268320 | tf_op jit(solution)/shard_map/ppermute | solution.py:13
  559.1 65.1 %all-reduce.22 = (f32[512,3]{0,1:T(4,128)S(1)}, f32[2,1024]{1,0:T(2,128)S(1)}, f32[6,512]{1,0:T(8,128)S(1)}) all-reduce(f32[512,3]{0,1:T(4,128)S(1)} %fusion.15, f32[2,1024]{1,0:T(2,128)S(1)} %pad_maximum_fusion.22, f32[6,512]{1,0:T(8,128)S(1)} %fusion.55), channel_id=1, replica_groups=mesh['dp'=16,'ctx'=8] {'dp'}, use_global_device_ids=true, to_apply=%region_0.1 | all-reduce | flops 6656 | bytes 53248 | tf_op jit(solution)/shard_map/psum | solution.py:229
  624.2 31.3 %all-reduce.23 = (f32[512,3]{0,1:T(4,128)}, f32[2,1024]{1,0:T(2,128)}, f32[6,512]{1,0:T(8,128)}) all-reduce(f32[512,3]{0,1:T(4,128)S(1)} %get-tuple-element.18, f32[2,1024]{1,0:T(2,128)S(1)} %get-tuple-element.19, f32[6,512]{1,0:T(8,128)S(1)} %get-tuple-element.20), channel_id=1, replica_groups=mesh['dp'=16,'ctx'=8] {'ctx'}, use_global_device_ids=true, to_apply=%region_1.2 | all-reduce | flops 6656 | bytes 53248 | tf_op jit(solution)/shard_map/psum | solution.py:228
  (146 shorter events, 72.1 us)
Async XLA Ops:
  7.2 175.3 %copy-start = (f32[6,512]{1,0:T(8,128)S(1)}, f32[6,512]{1,0:T(8,128)}, u32[]{:S(2)}) copy-start(f32[6,512]{1,0:T(8,128)} %param.18) | copy-start | bytes 36868
  7.2 57.8 %all-gather.8.cloned.1.call-start = ((), (), s32[]{:S(2)}) async-start(), calls=%async_computation.5 | async-start | bytes 3342336 | tf_op jit(solution)/shard_map/all_gather | solution.py:130
  9.1 102.0 %all-gather.6.cloned.1.call-start = ((), (), s32[]{:S(2)}) async-start(), calls=%async_computation.4 | async-start | bytes 1114112 | tf_op jit(solution)/shard_map/all_gather | solution.py:131
  9.8 167.3 %all-gather.10.cloned.1.call-start = ((), (), s32[]{:S(2)}) async-start(), calls=%async_computation.6 | async-start | bytes 3342336 | tf_op jit(solution)/shard_map/all_gather | solution.py:130
  10.5 270.1 %reduce-scatter.11.cloned.1.call-start = ((), (), s32[]{:S(2)}) async-start(), calls=%async_computation.10 | async-start | bytes 1114112 | tf_op jit(solution)/shard_map/reduce_scatter | solution.py:150
  13.7 99.3 %copy-start.3 = (bf16[512,512]{0,1:T(8,128)(2,1)}, bf16[512,512]{0,1:T(8,128)(2,1)S(1)}, u32[]{:S(2)}) copy-start(bf16[512,512]{0,1:T(8,128)(2,1)S(1)} %fusion.11) | copy-start | bytes 1572868
  13.8 9.4 %collective-permute-start = (bf16[512,131]{0,1:T(8,128)(2,1)S(1)}, bf16[512,131]{0,1:T(8,128)(2,1)S(1)}, u32[]{:S(2)}, u32[]{:S(2)}) collective-permute-start(bf16[512,131]{0,1:T(8,128)(2,1)S(1)} %get-tuple-element.76), channel_id=1, source_target_pairs={{0,1},{1,2},{2,3},{3,4},{4,5},{5,6},{6,7},{8,9},{9,10},{10,11},{11... | collective-permute-start | bytes 402440 | tf_op jit(solution)/shard_map/ppermute | solution.py:13
  17.2 7.1 %collective-permute-start.1 = (bf16[512,131]{0,1:T(8,128)(2,1)S(1)}, bf16[512,131]{0,1:T(8,128)(2,1)S(1)}, u32[]{:S(2)}, u32[]{:S(2)}) collective-permute-start(bf16[512,131]{0,1:T(8,128)(2,1)S(1)} %get-tuple-element.77), channel_id=1, source_target_pairs={{1,0},{2,1},{3,2},{4,3},{5,4},{6,5},{7,6},{9,8},{10,9},{11,10},{12... | collective-permute-start | bytes 402440 | tf_op jit(solution)/shard_map/ppermute | solution.py:13
  113.2 39.3 %collective-permute-start.4 = (bf16[512,512]{0,1:T(8,128)(2,1)S(1)}, bf16[512,512]{0,1:T(8,128)(2,1)S(1)}, u32[]{:S(2)}, u32[]{:S(2)}) collective-permute-start(bf16[512,512]{0,1:T(8,128)(2,1)S(1)} %fusion.25), channel_id=1, source_target_pairs={{1,0},{2,1},{3,2},{4,3},{5,4},{6,5},{7,6},{9,8},{10,9},{11,10},{12... | collective-permute-start | bytes 1572872 | tf_op jit(solution)/shard_map/ppermute | solution.py:13
  118.7 33.9 %collective-permute-start.3 = (bf16[512,512]{0,1:T(8,128)(2,1)S(1)}, bf16[512,512]{0,1:T(8,128)(2,1)S(1)}, u32[]{:S(2)}, u32[]{:S(2)}) collective-permute-start(bf16[512,512]{0,1:T(8,128)(2,1)S(1)} %fusion.25), channel_id=1, source_target_pairs={{0,1},{1,2},{2,3},{3,4},{4,5},{5,6},{6,7},{8,9},{9,10},{10,11},{11... | collective-permute-start | bytes 1572872 | tf_op jit(solution)/shard_map/ppermute | solution.py:13
  120.7 31.9 %collective-permute-start.2 = (bf16[512,259]{0,1:T(8,128)(2,1)S(1)}, bf16[512,259]{0,1:T(8,128)(2,1)S(1)}, u32[]{:S(2)}, u32[]{:S(2)}) collective-permute-start(bf16[512,259]{0,1:T(8,128)(2,1)S(1)} %get-tuple-element.74), channel_id=1, source_target_pairs={{0,2},{1,3},{2,4},{3,5},{4,6},{5,7},{8,10},{9,11},{10,12},{11,13},... | collective-permute-start | bytes 795656 | tf_op jit(solution)/shard_map/ppermute | solution.py:13
  124.1 28.4 %collective-permute-start.5 = (bf16[512,259]{0,1:T(8,128)(2,1)S(1)}, bf16[512,259]{0,1:T(8,128)(2,1)S(1)}, u32[]{:S(2)}, u32[]{:S(2)}) collective-permute-start(bf16[512,259]{0,1:T(8,128)(2,1)S(1)} %get-tuple-element.75), channel_id=1, source_target_pairs={{2,0},{3,1},{4,2},{5,3},{6,4},{7,5},{10,8},{11,9},{12,10},{13,11},... | collective-permute-start | bytes 795656 | tf_op jit(solution)/shard_map/ppermute | solution.py:13
  194.4 56.1 %collective-permute-start.6 = (f32[512,512]{0,1:T(8,128)}, f32[512,512]{0,1:T(8,128)S(1)}, u32[]{:S(2)}, u32[]{:S(2)}) collective-permute-start(f32[512,512]{0,1:T(8,128)} %get-tuple-element.30), channel_id=1, source_target_pairs={{1,0},{2,1},{3,2},{4,3},{5,4},{6,5},{7,6},{9,8},{10,9},{11,10},{12... | collective-permute-start | bytes 3145736 | tf_op jit(solution)/shard_map/ppermute | solution.py:13
  199.9 52.5 %collective-permute-start.7 = (f32[512,512]{0,1:T(8,128)}, f32[512,512]{0,1:T(8,128)}, u32[]{:S(2)}, u32[]{:S(2)}) collective-permute-start(f32[512,512]{0,1:T(8,128)} %get-tuple-element.31), channel_id=1, source_target_pairs={{0,1},{1,2},{2,3},{3,4},{4,5},{5,6},{6,7},{8,9},{9,10},{10,11},{11... | collective-permute-start | bytes 3145736 | tf_op jit(solution)/shard_map/ppermute | solution.py:13
  203.3 149.5 %reduce-scatter.9.cloned.1.call-start = ((), (), s32[]{:S(2)}) async-start(), calls=%async_computation.9 | async-start | bytes 2228224 | tf_op jit(solution)/shard_map/reduce_scatter | solution.py:150
  204.6 33.5 %collective-permute-start.8 = (f32[512,259]{0,1:T(8,128)S(1)}, f32[512,259]{0,1:T(8,128)S(1)}, u32[]{:S(2)}, u32[]{:S(2)}) collective-permute-start(f32[512,259]{0,1:T(8,128)S(1)} %get-tuple-element.32), channel_id=1, source_target_pairs={{2,0},{3,1},{4,2},{5,3},{6,4},{7,5},{10,8},{11,9},{12,10},{13,11},... | collective-permute-start | bytes 1591304 | tf_op jit(solution)/shard_map/ppermute | solution.py:13
  208.8 41.7 %collective-permute-start.9 = (f32[512,259]{0,1:T(8,128)S(1)}, f32[512,259]{0,1:T(8,128)S(1)}, u32[]{:S(2)}, u32[]{:S(2)}) collective-permute-start(f32[512,259]{0,1:T(8,128)S(1)} %get-tuple-element.33), channel_id=1, source_target_pairs={{0,2},{1,3},{2,4},{3,5},{4,6},{5,7},{8,10},{9,11},{10,12},{11,13},... | collective-permute-start | bytes 1591304 | tf_op jit(solution)/shard_map/ppermute | solution.py:13
  258.2 187.7 %reduce-scatter.7.cloned.1.call-start = ((), (), s32[]{:S(2)}) async-start(), calls=%async_computation.8 | async-start | bytes 6684672 | tf_op jit(solution)/shard_map/reduce_scatter | solution.py:150
  264.0 274.8 %reduce-scatter.5.cloned.1.call-start = ((), (), s32[]{:S(2)}) async-start(), calls=%async_computation.7 | async-start | bytes 6684672 | tf_op jit(solution)/shard_map/reduce_scatter | solution.py:150
  273.7 381.8 %all-reduce.27.cloned.1.call-start = ((), (), s32[]{:S(2)}) async-start(), calls=%async_computation.11 | async-start | bytes 1966080 | tf_op jit(solution)/shard_map/psum | solution.py:149
  280.6 267.1 %copy-start.17 = (bf16[512,512]{0,1:T(8,128)(2,1)S(1)}, bf16[512,512]{0,1:T(8,128)(2,1)}, u32[]{:S(2)}) copy-start(bf16[512,512]{0,1:T(8,128)(2,1)} %copy-done.16) | copy-start | bytes 1572868
  538.9 10.2 %collective-permute-start.10 = (f32[512,131]{0,1:T(8,128)S(1)}, f32[512,131]{0,1:T(8,128)S(1)}, u32[]{:S(2)}, u32[]{:S(2)}) collective-permute-start(f32[512,131]{0,1:T(8,128)S(1)} %get-tuple-element.70), channel_id=1, source_target_pairs={{1,0},{2,1},{3,2},{4,3},{5,4},{6,5},{7,6},{9,8},{10,9},{11,10},{12... | collective-permute-start | bytes 804872 | tf_op jit(solution)/shard_map/ppermute | solution.py:13
  544.5 13.7 %collective-permute-start.11 = (f32[512,131]{0,1:T(8,128)S(1)}, f32[512,131]{0,1:T(8,128)S(1)}, u32[]{:S(2)}, u32[]{:S(2)}) collective-permute-start(f32[512,131]{0,1:T(8,128)S(1)} %get-tuple-element.71), channel_id=1, source_target_pairs={{0,1},{1,2},{2,3},{3,4},{4,5},{5,6},{6,7},{8,9},{9,10},{10,11},{11... | collective-permute-start | bytes 804872 | tf_op jit(solution)/shard_map/ppermute | solution.py:13
  558.3 102.3 %copy-start.1 = (f32[6,512]{1,0:T(8,128)S(1)}, f32[6,512]{1,0:T(8,128)}, u32[]{:S(2)}) copy-start(f32[6,512]{1,0:T(8,128)} %param.18) | copy-start | bytes 36868
  (32 other events, 385.2 us)
Sparse Core Ops, SparseCore 0:
  11.0 53.9 all-gather.7
  67.4 43.6 all-gather.5
  113.4 63.5 all-gather.9
  203.4 75.1 reduce-scatter.10
  282.9 69.8 reduce-scatter.8
  357.4 88.4 reduce-scatter.6
  450.6 88.1 reduce-scatter.4
  541.8 75.4 all-reduce.26
